TPU v7x, 32 devices: a whole 2x2x4 slice. The times are simulated.
32 devices in a mesh: light: 4 (over z), pix: 4 (over x, core), cam: 2 (over y).
Axes of the slice: x: 2, y: 2, z: 4, core: 2. Of those that a mesh axis runs over, the one named last changes fastest.
Arguments:
- reflectance: bfloat16 [1024, 32, 4096], P('light', 'cam', 'pix'), may hold values from -120 to 120
- start_basis: float32 [1024, 128], replicated, may hold values from -6 to 6
Outputs:
- core_tensor: float32 [128, 32, 4096], P('light', 'cam', 'pix')
- light_basis: float32 [1024, 128], P('light')
All inputs are finite; a program needn't handle non-finite values.
Results may differ from a plain program's by a relative error of at most 0.015.
Values may be sent and summed in bfloat16 or wider, within the bound.
A program may use at most 128 MiB of HBM per device.

v0:
```python
import jax
import jax.numpy as jnp
from jax import lax
from jax.sharding import PartitionSpec as P

ITERS = 2


def orthonormal(image_full):
    inner_gram = jnp.dot(
        image_full.T,
        image_full,
        preferred_element_type=jnp.float32,
        precision=lax.Precision.HIGHEST,
    )
    factor = jnp.linalg.cholesky(inner_gram)
    return lax.linalg.triangular_solve(
        factor, image_full, left_side=False, lower=True, transpose_a=True
    )


def per_device(reflectance, start_basis):
    light_rows, camera_cols, pixels = reflectance.shape
    rank_total = start_basis.shape[1]
    light_count = lax.axis_size("light")
    position = lax.axis_index("light")
    inverse_cols = 1.0 / (camera_cols * pixels * lax.axis_size("cam") * lax.axis_size("pix"))
    fibers = reflectance.reshape(light_rows, camera_cols * pixels)
    full_gram = None
    exchanged = None
    exchanged = lax.all_to_all(reflectance, "light", split_axis=2, concat_axis=0, tiled=True)
    gathered = exchanged.reshape(light_rows * light_count, -1)
    own_gram = lax.dot_general(
        gathered, gathered, (((1,), (1,)), ((), ())), preferred_element_type=jnp.float32
    )
    full_gram = lax.psum(own_gram, ("light", "pix", "cam")) * inverse_cols
    gram_rows = lax.dynamic_slice_in_dim(full_gram, position * light_rows, light_rows, 0)
    basis_now = start_basis
    for iteration in range(ITERS):
        image_rows = jnp.dot(
            gram_rows,
            basis_now,
            preferred_element_type=jnp.float32,
            precision=lax.Precision.HIGHEST,
        )
        image_full = lax.all_gather(
            image_rows.astype(jnp.bfloat16), "light", axis=0, tiled=True
        ).astype(image_rows.dtype)
        basis_now = orthonormal(image_full)
    basis_rows = lax.dynamic_slice_in_dim(basis_now, position * light_rows, light_rows, 0)
    rank_rows = rank_total // light_count
    rounded = basis_rows.astype(jnp.bfloat16)
    core_rows = lax.psum_scatter(
        lax.dot_general(
            rounded, fibers, (((0,), (0,)), ((), ())), preferred_element_type=jnp.float32
        ).astype(jnp.bfloat16),
        "light",
        scatter_dimension=0,
        tiled=True,
    ).astype(jnp.float32)
    return (core_rows.reshape(rank_rows, camera_cols, pixels), basis_rows)


def solution(mesh):
    placed = (P("light", "cam", "pix"), P())
    return jax.shard_map(
        per_device,
        mesh=mesh,
        in_specs=placed,
        out_specs=(P("light", "cam", "pix"), P("light", None)),
        check_vma=False,
    )
```

profile of v0, /device:TPU:0, one launch (start us, length us, event | category | flops | bytes accessed | tf_op | source)
XLA Modules:
  0.0 573.0 jit_solution(15910480420709180516)
XLA Ops:
  7.2 0.0 all-reduce.2.cloned.1.call-start
  7.2 13.4 %copy.16 = bf16[256,16,1024]{0,1,2:T(8,128)(2,1)} copy(bf16[256,16,1024]{2,1,0:T(8,128)(2,1)} %param.5) | data formatting | bytes 16777216 | tf_op args[0]
  20.7 192.2 %all_to_all.15 = bf16[256,16,1024]{0,1,2:T(8,128)(2,1)} all-to-all(bf16[256,16,1024]{0,1,2:T(8,128)(2,1)} %copy.16), channel_id=1, replica_groups=mesh['light'=4,'pix'=4,'cam'=2] {'light'}, dimensions={2} | all-to-all | bytes 16777216 | tf_op jit(solution)/shard_map/all_to_all | solution.py:31
  212.9 16.0 %copy.17 = bf16[256,16,4,256]{3,1,0,2:T(8,128)(2,1)} copy(bf16[256,16,4,256]{0,1,3,2:T(8,128)(2,1)} %bitcast.43) | data formatting | bytes 16777216 | tf_op jit(solution)/shard_map/all_to_all | solution.py:31
  228.9 12.2 %copy.21 = bf16[128,8,16,256]{3,1,2,0:T(8,128)(2,1)} copy(bf16[128,8,16,256]{3,2,1,0:T(8,128)(2,1)} %bitcast.44) | data formatting | bytes 16777216
  241.1 16.0 %fusion.17 = f32[1024,1024]{1,0:T(8,128)} fusion(bf16[1024,4096]{1,0:T(8,128)(2,1)} %bitcast.45), kind=kOutput, calls=%fused_computation.33 | convolution fusion | flops 8589934592 | bytes 12582912 | tf_op jit(solution)/shard_map/dot_general | solution.py:33
  257.1 0.0 all-reduce.2.cloned.1.call-update
  257.1 0.5 reduce-scatter.2.cloned.1.call-start
  257.7 15.6 %copy.22 = bf16[32,8,16,1024]{3,1,2,0:T(8,128)(2,1)} copy(bf16[32,8,16,1024]{3,2,1,0:T(8,128)(2,1)} %bitcast.41) | data formatting | bytes 16777216
  273.3 125.7 %all-reduce.2.cloned.1.call-done = f32[1024,1024]{1,0:T(8,128)} async-done(((f32[1024,1024]{1,0:T(8,128)}), f32[1024,1024]{1,0:T(8,128)}) %all-reduce.2.cloned.1.call-update) | async-done | bytes 4194320 | tf_op jit(solution)/shard_map/psum | solution.py:36
  399.0 2.2 convolution_convert_fusion.2
  401.2 14.5 %all_gather.6 = bf16[1024,128]{1,0:T(8,128)(2,1)S(1)} all-gather(bf16[256,128]{1,0:T(8,128)(2,1)S(1)} %convolution_convert_fusion.2), channel_id=1, replica_groups=mesh['light'=4,'pix'=4,'cam'=2] {'light'}, dimensions={0}, use_global_device_ids=true | all-gather | bytes 327680 | tf_op jit(solution)/shard_map/all_gather | solution.py:46
  415.7 0.3 fusion.18
  416.0 0.1 copy.18
  416.1 11.7 %cholesky.44 = f32[128,128]{1,0:T(8,128)S(1)} custom-call(f32[128,128]{1,0:T(8,128)S(1)} %fusion.9), custom_call_target="Cholesky" | custom-call | tf_op jit(solution)/shard_map/jit(cholesky)/cholesky | solution.py:16
  427.9 0.6 compare_reduce_fusion.1
  428.5 0.7 fusion.4
  429.2 9.8 %custom-call.6 = f32[1,128,128]{1,2,0:T(8,128)S(1)} custom-call(f32[1,128,128]{2,1,0:T(8,128)S(1)} %fusion.4), custom_call_target="InvertDiagBlocksLowerTriangular" | custom-call | tf_op jit(solution)/shard_map/triangular_solve/custom-call.0 | solution.py:17
  439.0 0.6 convolution_bitcast_fusion.1
  439.6 2.2 convolution_convert_fusion.1
  441.8 14.5 %all_gather.7 = bf16[1024,128]{1,0:T(8,128)(2,1)S(1)} all-gather(bf16[256,128]{1,0:T(8,128)(2,1)S(1)} %convolution_convert_fusion.1), channel_id=1, replica_groups=mesh['light'=4,'pix'=4,'cam'=2] {'light'}, dimensions={0}, use_global_device_ids=true | all-gather | bytes 327680 | tf_op jit(solution)/shard_map/all_gather | solution.py:46
  456.3 0.3 fusion.19
  456.6 0.1 copy.19
  456.7 11.7 %cholesky.55 = f32[128,128]{1,0:T(8,128)S(1)} custom-call(f32[128,128]{1,0:T(8,128)S(1)} %fusion.7), custom_call_target="Cholesky" | custom-call | tf_op jit(solution)/shard_map/jit(cholesky)/cholesky | solution.py:16
  468.4 0.6 compare_reduce_fusion
  469.1 0.7 fusion.5
  469.7 9.8 %custom-call.7 = f32[1,128,128]{1,2,0:T(8,128)S(1)} custom-call(f32[1,128,128]{2,1,0:T(8,128)S(1)} %fusion.5), custom_call_target="InvertDiagBlocksLowerTriangular" | custom-call | tf_op jit(solution)/shard_map/triangular_solve/custom-call.0 | solution.py:17
  479.6 0.6 convolution_bitcast_fusion
  480.2 6.6 %convolution_convert_fusion = bf16[128,16384]{1,0:T(8,128)(2,1)} fusion(bf16[256,16384]{1,0:T(8,128)(2,1)} %bitcast.42, f32[256,128]{0,1:T(8,128)S(1)} %constant_dynamic-slice_fusion), kind=kOutput, calls=%fused_computation | convolution fusion | flops 1075871744 | bytes 12713984 | tf_op jit(solution)/shard_map/dot_general | solution.py:54
  486.9 0.8 copy.20
  487.6 75.2 %reduce-scatter.2.cloned.1.call-done = bf16[32,16384]{1,0:T(8,128)(2,1)} async-done(((bf16[128,16384]{1,0:T(8,128)(2,1)}), bf16[32,16384]{1,0:T(8,128)(2,1)}) %reduce-scatter.2.cloned.1.call-update) | async-done | bytes 1048592 | tf_op jit(solution)/shard_map/reduce_scatter | solution.py:53
  562.8 3.2 copy.23
  (8 shorter events, 0.1 us)
Async XLA Ops:
  7.2 391.9 %copy-start = (f32[1024,128]{1,0:T(8,128)S(1)}, f32[1024,128]{1,0:T(8,128)}, u32[]{:S(2)}) copy-start(f32[1024,128]{1,0:T(8,128)} %param.6) | copy-start | bytes 1572868
  7.2 391.8 %all-reduce.2.cloned.1.call-start = ((), (), s32[]{:S(2)}) async-start(), calls=%async_computation.2 | async-start | bytes 8388608 | tf_op jit(solution)/shard_map/psum | solution.py:36
  257.1 305.7 %reduce-scatter.2.cloned.1.call-start = ((), (), s32[]{:S(2)}) async-start(), calls=%async_computation.3 | async-start | bytes 5242880 | tf_op jit(solution)/shard_map/reduce_scatter | solution.py:53
Sparse Core Ops, SparseCore 0:
  257.3 141.7 all-reduce.1
  487.0 75.7 reduce-scatter.1
where the time goes:
time: 582 us; the launch traced here: 573 us
  blocking collectives  221 us (38%)
  waiting for transfers between devices  201 us (35%)
  local copies, waits for them, and re-layouts  61.5 us (11%)
  other arithmetic  45.7 us (8%)
  matrix products  28.8 us (5%)
  between operations  14.4 us (2%)
    all_to_all x1, blocking collectives, per_device(): lax.all_to_all(reflectance, 'light', split_axis=2, concat_axis=0, tiled=T...  192 us
    psum x1, waiting for transfers between devices, per_device(): full_gram = lax.psum(own_gram, ('light', 'pix', 'cam')) * inverse_cols  126 us
    reduce_scatter x1, waiting for transfers between devices, per_device(): lax.psum_scatter(lax.dot_general(rounded, fibers, (((0,), (0,)), ((), ())...  75.2 us
    unnamed x7, local copies, waits for them, and re-layouts  45.2 us
    all_gather x2, blocking collectives, per_device(): lax.all_gather(image_rows.astype(jnp.bfloat16), 'light', axis=0, tiled=True)  28.9 us
    another operation x6, other arithmetic, orthonormal(): factor = jnp.linalg.cholesky(inner_gram)  24.8 us
    another operation x4, other arithmetic, orthonormal(): lax.linalg.triangular_solve(factor, image_full, left_side=False, lower=Tr...  20.9 us
    all_to_all x1, local copies, waits for them, and re-layouts, per_device(): lax.all_to_all(reflectance, 'light', split_axis=2, concat_axis=0, tiled=T...  16 us
  transfers between devices with their start and end apart: 2, of which 2 were waited for; matrix products, arithmetic and copies ran while one was open for 3% of the time, Pallas kernels for 0%

commit v1 on v0

--- a/solution.py
+++ b/solution.py
@@ -4,6 +4,13 @@
 from jax.sharding import PartitionSpec as P
 
 ITERS = 2
+
+
+def swap_blocks(x, mesh_axis, split, join):
+    size = lax.axis_size(mesh_axis)
+    parts = jnp.stack(jnp.split(x, size, axis=split), axis=0)
+    parts = lax.all_to_all(parts, mesh_axis, split_axis=0, concat_axis=0)
+    return jnp.concatenate(parts, axis=join)
 
 
 def orthonormal(image_full):
@@ -28,7 +35,7 @@
     fibers = reflectance.reshape(light_rows, camera_cols * pixels)
     full_gram = None
     exchanged = None
-    exchanged = lax.all_to_all(reflectance, "light", split_axis=2, concat_axis=0, tiled=True)
+    exchanged = swap_blocks(reflectance, "light", 2, 0)
     gathered = exchanged.reshape(light_rows * light_count, -1)
     own_gram = lax.dot_general(
         gathered, gathered, (((1,), (1,)), ((), ())), preferred_element_type=jnp.float32

time: 582 us -> 554 us (0.952)
  local copies, waits for them, and re-layouts: 61.5 us -> 35.9 us
    all_to_all x1 -> x0, local copies, waits for them, and re-layouts: 16 us -> none  [per_device(): lax.all_to_all(reflectance, 'light', split_axis=2, concat_axis=0, tiled=T...]
    unnamed x7 -> x6, local copies, waits for them, and re-layouts: 45.2 us -> 31.8 us
where the time goes in v1:
time: 554 us; the launch traced here: 546 us
  blocking collectives  218 us (39%)
  waiting for transfers between devices  201 us (36%)
  other arithmetic  46.9 us (8%)
  local copies, waits for them, and re-layouts  35.9 us (6%)
  matrix products  28.8 us (5%)
  between operations  14.4 us (3%)
    all_to_all x1, blocking collectives, swap_blocks(): parts = lax.all_to_all(parts, mesh_axis, split_axis=0, concat_axis=0)  189 us
    psum x1, waiting for transfers between devices, per_device(): full_gram = lax.psum(own_gram, ('light', 'pix', 'cam')) * inverse_cols  126 us
    reduce_scatter x1, waiting for transfers between devices, per_device(): lax.psum_scatter(lax.dot_general(rounded, fibers, (((0,), (0,)), ((), ())...  75.2 us
    unnamed x6, local copies, waits for them, and re-layouts  31.8 us
    all_gather x2, blocking collectives, per_device(): lax.all_gather(image_rows.astype(jnp.bfloat16), 'light', axis=0, tiled=True)  28.9 us
    another operation x6, other arithmetic, orthonormal(): factor = jnp.linalg.cholesky(inner_gram)  24.8 us
    another operation x4, other arithmetic, orthonormal(): lax.linalg.triangular_solve(factor, image_full, left_side=False, lower=Tr...  20.9 us
    dot_general x1, matrix products, per_device(): lax.dot_general(gathered, gathered, (((1,), (1,)), ((), ())), preferred_e...  16 us
  transfers between devices with their start and end apart: 2, of which 2 were waited for; matrix products, arithmetic and copies ran while one was open for 3% of the time, Pallas kernels for 0%

profile of v1, /device:TPU:0, one launch (start us, length us, event | category | flops | bytes accessed | tf_op | source)
XLA Modules:
  0.0 546.2 jit_solution(12962379802645633339)
XLA Ops:
  7.2 0.0 all-reduce.2.cloned.1.call-start
  7.2 3.9 slice_bitcast_fusion.3
  11.2 1.1 pad_maximum_fusion
  12.3 189.3 %all_to_all.5 = bf16[4,256,16,256]{3,2,1,0:T(8,128)(2,1)} all-to-all(bf16[4,256,16,256]{3,2,1,0:T(8,128)(2,1)S(1)} %pad_maximum_fusion), channel_id=1, replica_groups=mesh['light'=4,'pix'=4,'cam'=2] {'light'}, dimensions={0} | all-to-all | bytes 16777216 | tf_op jit(solution)/shard_map/all_to_all | solution.py:12
  201.6 12.2 %copy.7 = bf16[128,8,16,256]{3,1,2,0:T(8,128)(2,1)} copy(bf16[128,8,16,256]{3,2,1,0:T(8,128)(2,1)} %bitcast.49) | data formatting | bytes 16777216
  213.8 16.0 %fusion.17 = f32[1024,1024]{1,0:T(8,128)} fusion(bf16[1024,4096]{1,0:T(8,128)(2,1)} %bitcast.50), kind=kOutput, calls=%fused_computation.38 | convolution fusion | flops 8589934592 | bytes 12582912 | tf_op jit(solution)/shard_map/dot_general | solution.py:40
  229.8 0.0 all-reduce.2.cloned.1.call-update
  229.8 0.5 reduce-scatter.2.cloned.1.call-start
  230.3 15.6 %copy.8 = bf16[32,8,16,1024]{3,1,2,0:T(8,128)(2,1)} copy(bf16[32,8,16,1024]{3,2,1,0:T(8,128)(2,1)} %bitcast.47) | data formatting | bytes 16777216
  246.0 126.2 %all-reduce.2.cloned.1.call-done = f32[1024,1024]{1,0:T(8,128)} async-done(((f32[1024,1024]{1,0:T(8,128)}), f32[1024,1024]{1,0:T(8,128)}) %all-reduce.2.cloned.1.call-update) | async-done | bytes 4194320 | tf_op jit(solution)/shard_map/psum | solution.py:43
  372.2 2.2 convolution_convert_fusion.2
  374.4 14.5 %all_gather.6 = bf16[1024,128]{1,0:T(8,128)(2,1)S(1)} all-gather(bf16[256,128]{1,0:T(8,128)(2,1)S(1)} %convolution_convert_fusion.2), channel_id=1, replica_groups=mesh['light'=4,'pix'=4,'cam'=2] {'light'}, dimensions={0}, use_global_device_ids=true | all-gather | bytes 327680 | tf_op jit(solution)/shard_map/all_gather | solution.py:53
  388.9 0.3 fusion.18
  389.1 0.1 copy.4
  389.2 11.7 %cholesky.44 = f32[128,128]{1,0:T(8,128)S(1)} custom-call(f32[128,128]{1,0:T(8,128)S(1)} %fusion.9), custom_call_target="Cholesky" | custom-call | tf_op jit(solution)/shard_map/jit(cholesky)/cholesky | solution.py:23
  401.0 0.6 compare_reduce_fusion.1
  401.6 0.7 fusion.4
  402.3 9.8 %custom-call.6 = f32[1,128,128]{1,2,0:T(8,128)S(1)} custom-call(f32[1,128,128]{2,1,0:T(8,128)S(1)} %fusion.4), custom_call_target="InvertDiagBlocksLowerTriangular" | custom-call | tf_op jit(solution)/shard_map/triangular_solve/custom-call.0 | solution.py:24
  412.1 0.6 convolution_bitcast_fusion.1
  412.7 2.2 convolution_convert_fusion.1
  415.0 14.5 %all_gather.7 = bf16[1024,128]{1,0:T(8,128)(2,1)S(1)} all-gather(bf16[256,128]{1,0:T(8,128)(2,1)S(1)} %convolution_convert_fusion.1), channel_id=1, replica_groups=mesh['light'=4,'pix'=4,'cam'=2] {'light'}, dimensions={0}, use_global_device_ids=true | all-gather | bytes 327680 | tf_op jit(solution)/shard_map/all_gather | solution.py:53
  429.4 0.3 fusion.19
  429.7 0.1 copy.5
  429.8 11.7 %cholesky.55 = f32[128,128]{1,0:T(8,128)S(1)} custom-call(f32[128,128]{1,0:T(8,128)S(1)} %fusion.7), custom_call_target="Cholesky" | custom-call | tf_op jit(solution)/shard_map/jit(cholesky)/cholesky | solution.py:23
  441.6 0.6 compare_reduce_fusion
  442.2 0.7 fusion.5
  442.9 9.8 %custom-call.7 = f32[1,128,128]{1,2,0:T(8,128)S(1)} custom-call(f32[1,128,128]{2,1,0:T(8,128)S(1)} %fusion.5), custom_call_target="InvertDiagBlocksLowerTriangular" | custom-call | tf_op jit(solution)/shard_map/triangular_solve/custom-call.0 | solution.py:24
  452.7 0.6 convolution_bitcast_fusion
  453.3 6.6 %convolution_convert_fusion = bf16[128,16384]{1,0:T(8,128)(2,1)} fusion(bf16[256,16384]{1,0:T(8,128)(2,1)} %bitcast.48, f32[256,128]{0,1:T(8,128)S(1)} %constant_dynamic-slice_fusion), kind=kOutput, calls=%fused_computation | convolution fusion | flops 1075871744 | bytes 12713984 | tf_op jit(solution)/shard_map/dot_general | solution.py:61
  460.0 0.8 copy.6
  460.7 75.2 %reduce-scatter.2.cloned.1.call-done = bf16[32,16384]{1,0:T(8,128)(2,1)} async-done(((bf16[128,16384]{1,0:T(8,128)(2,1)}), bf16[32,16384]{1,0:T(8,128)(2,1)}) %reduce-scatter.2.cloned.1.call-update) | async-done | bytes 1048592 | tf_op jit(solution)/shard_map/reduce_scatter | solution.py:60
  535.9 3.2 copy.9
  (8 shorter events, 0.1 us)
Async XLA Ops:
  7.2 365.0 %copy-start = (f32[1024,128]{1,0:T(8,128)S(1)}, f32[1024,128]{1,0:T(8,128)}, u32[]{:S(2)}) copy-start(f32[1024,128]{1,0:T(8,128)} %param.6) | copy-start | bytes 1572868
  7.2 365.0 %all-reduce.2.cloned.1.call-start = ((), (), s32[]{:S(2)}) async-start(), calls=%async_computation.2 | async-start | bytes 8388608 | tf_op jit(solution)/shard_map/psum | solution.py:43
  229.8 306.1 %reduce-scatter.2.cloned.1.call-start = ((), (), s32[]{:S(2)}) async-start(), calls=%async_computation.3 | async-start | bytes 5242880 | tf_op jit(solution)/shard_map/reduce_scatter | solution.py:60
Sparse Core Ops, SparseCore 0:
  229.9 142.1 all-reduce.1
  460.1 75.7 reduce-scatter.1
